TPU v7x, 768 devices: a whole 4x8x12 slice. The times are simulated.
768 devices in a mesh: section: 16 (over x, y_hi, core), tp: 48 (over y_lo, z).
Axes of the slice: x: 4, y: 8 (y_hi: 2, y_lo: 4; y = y_hi * 4 + y_lo), z: 12, core: 2. Of those that a mesh axis runs over, the one named last changes fastest.
Arguments:
- grad_attn: bfloat16 [16, 48, 128, 128], P('section', 'tp'), may hold values from -6 to 6
- w_value: bfloat16 [16, 12288, 6144], P('section', 'tp'), may hold values from -0.0546875 to 0.0546875
- probs_own: bfloat16 [16, 48, 128, 128], P('section', 'tp'), may hold values from 0.0009994507 to 0.25
- probs_spare: bfloat16 [16, 48, 128, 128], P('section', 'tp'), may hold values from 0.0009994507 to 0.25
- evicted: int32 [16, 4], P('section'), may hold values from 0 to 1, as said below
- layer_input: bfloat16 [16, 128, 12288], P('section', None, 'tp'), may hold values from -6 to 6
- gain: float32 [16, 12288], P('section', 'tp'), may hold values from 0.1 to 1.9
Outputs:
- handed: bfloat16 [16, 128, 12288], P('section', None, 'tp')
Inputs may be any that keep to these rules, and one draw needn't show every extreme that they name: Section 0 has every tile evicted.
All inputs are finite; a program needn't handle non-finite values.
Results may differ from a plain program's by a relative error of at most 0.0049.
Values may be sent and summed in bfloat16 or wider, within the bound.
A program may use at most 32 MiB of HBM per device.

v0:
```python
import jax
import jax.numpy as jnp
from jax import lax
from jax.sharding import PartitionSpec as P

D = 12288


def passed_along(block, axis, distance):
    devices = range(lax.axis_size(axis))
    route = [((i - distance) % len(devices), i) for i in devices]
    return lax.ppermute(block, axis, route)


def per_device(grad_attn, w_value, probs_own, probs_spare, evicted, layer_input, gain):
    sections = lax.axis_size("section")
    fetched = probs_spare
    fetched = passed_along(fetched, "section", sections // 2)
    tokens = probs_own.shape[2]
    head_size = grad_attn.shape[3]
    flags = jnp.repeat(evicted[0], tokens // evicted.shape[1])
    mixed = jnp.where(flags[None, :, None] == 1, fetched[0], probs_own[0])
    weights = w_value[0]
    features = weights.shape[0]
    values = layer_input[0].astype(jnp.float32)
    scales = gain[0]
    squares = lax.psum(jnp.sum(values * values, axis=1), "tp")
    grads = jnp.einsum(
        "hqk,hqd->hkd",
        lax.all_gather(mixed, "tp", axis=0, tiled=True),
        lax.all_gather(grad_attn[0], "tp", axis=0, tiled=True),
        preferred_element_type=jnp.float32,
    ).astype(jnp.bfloat16)
    count = grads.shape[0]
    columns = weights
    columns = columns.reshape(features, count, head_size)
    grad_normed = jnp.einsum("hkd,fhd->kf", grads, columns, preferred_element_type=jnp.float32)
    local_inner = jnp.sum(scales[None, :] * grad_normed * values, axis=1)
    inner = lax.psum(local_inner, "tp")
    inv = 1.0 / jnp.sqrt(squares / D + 1e-05)
    branch = scales[None, :] * grad_normed * inv[:, None] - values * (inner * inv**3 / D)[:, None]
    branch = branch.astype(jnp.bfloat16)[None]
    return passed_along(branch, "section", -1)


def solution(mesh):
    in_specs = (
        P("section", "tp", None, None),
        P("section", "tp", None),
        P("section", "tp", None, None),
        P("section", "tp", None, None),
        P("section", None),
        P("section", None, "tp"),
        P("section", "tp"),
    )
    out_specs = P("section", None, "tp")
    return jax.shard_map(
        per_device, mesh=mesh, in_specs=in_specs, out_specs=out_specs, check_vma=False
    )
```

profile of v0, /device:TPU:1, one launch (start us, length us, event | category | flops | bytes accessed | tf_op | source)
XLA Modules:
  0.0 599.5 jit_solution(14417247292480483543)
XLA Ops:
  6.5 0.0 all-gather.6.cloned.1.call-start
  6.5 0.7 all-gather.6.cloned.1.call-update
  7.3 0.0 all-gather.4.cloned.1.call-start
  7.3 5.5 collective-permute-start
  12.8 0.7 compare_bitcast_fusion
  13.5 0.1 broadcast_in_dim.16
  13.5 0.1 eq.21
  13.6 0.7 collective-permute-done
  14.3 1.5 bitcast_select_fusion
  15.8 0.0 all-gather.4.cloned.1.call-update
  15.8 0.0 copy-start
  15.8 0.0 copy-start.1
  15.8 2.6 copy.10
  18.4 194.1 %all-gather.6.cloned.1.call-done = bf16[48,1,128,128]{3,2,1,0:T(8,128)(2,1)} async-done(((bf16[1,1,128,128]{3,2,1,0:T(8,128)(2,1)}), bf16[48,1,128,128]{3,2,1,0:T(8,128)(2,1)}) %all-gather.6.cloned.1.call-update) | async-done | bytes 1572880 | tf_op jit(solution)/shard_map/all_gather | solution.py:31
  212.5 221.6 %all-gather.4.cloned.1.call-done = bf16[48,128,128]{2,1,0:T(8,128)(2,1)} async-done(((bf16[1,128,128]{2,1,0:T(8,128)(2,1)}), bf16[48,128,128]{2,1,0:T(8,128)(2,1)}) %all-gather.4.cloned.1.call-update) | async-done | bytes 1572880 | tf_op jit(solution)/shard_map/all_gather | solution.py:30
  434.1 0.0 copy-done
  434.1 0.0 copy-done.1
  434.1 3.7 fusion.15
  437.8 94.7 %all-reduce = (f32[128]{0:T(128)S(1)}, f32[128]{0:T(128)S(1)}) all-reduce(f32[128]{0:T(128)S(1)} %get-tuple-element.6, f32[128]{0:T(128)S(1)} %get-tuple-element.5), channel_id=1, replica_groups=mesh['section'=16,'tp'=48] {'tp'}, use_global_device_ids=true, to_apply=%region_3.4 | all-reduce | flops 256 | bytes 2048 | tf_op jit(solution)/shard_map/psum | solution.py:39
  532.5 0.1 fusion.19
  532.6 55.2 %collective-permute-start.1 = (bf16[1,128,256]{2,1,0:T(8,128)(2,1)S(1)}, bf16[1,128,256]{2,1,0:T(8,128)(2,1)S(1)}, u32[]{:S(2)}, u32[]{:S(2)}) collective-permute-start(bf16[1,128,256]{2,1,0:T(8,128)(2,1)S(1)} %fusion.19), channel_id=1, source_target_pairs={{48,0},{96,48},{144,96},{192,144},{240,192},{288,240},{336,288},{3... | collective-permute-start | bytes 196616 | tf_op jit(solution)/shard_map/ppermute | solution.py:12
  587.8 4.3 collective-permute-done.1
  592.1 0.6 copy.20
  (1 shorter events, 0.0 us)
Async XLA Ops:
  6.5 206.0 %all-gather.6.cloned.1.call-start = ((), (), s32[]{:S(2)}) async-start(), calls=%async_computation.1 | async-start | bytes 1605632 | tf_op jit(solution)/shard_map/all_gather | solution.py:31
  7.3 426.8 %all-gather.4.cloned.1.call-start = ((), (), s32[]{:S(2)}) async-start(), calls=%async_computation | async-start | bytes 1605632 | tf_op jit(solution)/shard_map/all_gather | solution.py:30
  7.3 7.0 %collective-permute-start = (bf16[1,1,128,128]{3,2,1,0:T(8,128)(2,1)}, bf16[1,1,128,128]{3,2,1,0:T(8,128)(2,1)S(1)}, u32[]{:S(2)}, u32[]{:S(2)}) collective-permute-start(bf16[1,1,128,128]{3,2,1,0:T(8,128)(2,1)} %param.10), channel_id=1, source_target_pairs={{384,0},{432,48},{480,96},{528,144},{576,192},{624,240},{672,288},... | collective-permute-start | bytes 98312 | tf_op jit(solution)/shard_map/ppermute | solution.py:12
  15.8 418.3 %copy-start = (bf16[1,128,256]{2,1,0:T(8,128)(2,1)S(1)}, bf16[1,128,256]{2,1,0:T(8,128)(2,1)}, u32[]{:S(2)}) copy-start(bf16[1,128,256]{2,1,0:T(8,128)(2,1)} %param.12) | copy-start | bytes 196612
  15.8 418.3 %copy-start.1 = (f32[1,256]{1,0:T(1,128)S(1)}, f32[1,256]{1,0:T(1,128)}, u32[]{:S(2)}) copy-start(f32[1,256]{1,0:T(1,128)} %param.13) | copy-start | bytes 3076
  532.6 59.5 %collective-permute-start.1 = (bf16[1,128,256]{2,1,0:T(8,128)(2,1)S(1)}, bf16[1,128,256]{2,1,0:T(8,128)(2,1)S(1)}, u32[]{:S(2)}, u32[]{:S(2)}) collective-permute-start(bf16[1,128,256]{2,1,0:T(8,128)(2,1)S(1)} %fusion.19), channel_id=1, source_target_pairs={{48,0},{96,48},{144,96},{192,144},{240,192},{288,240},{336,288},{3... | collective-permute-start | bytes 196616 | tf_op jit(solution)/shard_map/ppermute | solution.py:12
Sparse Core Ops, SparseCore 0:
  9.7 202.7 all-gather.5
  214.9 219.1 all-gather.3
where the time goes:
time: 600 us
  waiting for transfers between devices  421 us (70%)
  blocking collectives  94.7 us (16%)
  starting transfers between devices  60.7 us (10%)
  between operations  13.5 us (2%)
    all_gather x1, waiting for transfers between devices, per_device(): lax.all_gather(mixed, 'tp', axis=0, tiled=True)  222 us
    all_gather x1, waiting for transfers between devices, per_device(): lax.all_gather(grad_attn[0], 'tp', axis=0, tiled=True)  194 us
    psum x1, blocking collectives, per_device(): inner = lax.psum(local_inner, 'tp')  94.7 us
    ppermute x2, starting transfers between devices, passed_along(): return lax.ppermute(block, axis, route)  60.6 us
  transfers between devices with their start and end apart: 4, of which 4 were waited for; matrix products, arithmetic and copies ran while one was open for 1% of the time, Pallas kernels for 0%

commit v1 on v0

v1 whole, which is shorter than its diff:
```python
import functools

import jax
import jax.numpy as jnp
from jax import lax
from jax.experimental import pallas as pl
from jax.experimental.pallas import tpu as pltpu
from jax.sharding import PartitionSpec as P

RUN = 4
MESH = pl.DeviceIdType.MESH


def kernel(
    sizes,
    ga_h,
    w_h,
    own_h,
    spare_h,
    ev_h,
    x_h,
    gain_h,
    out_ref,
    ga_v,
    w_v,
    own_v,
    spare_v,
    ev_s,
    x_v,
    gain_v,
    xr_v,
    gath,
    acc,
    a_send,
    a_recv,
    red_loc,
    red_y,
    red_col,
    red_z,
    lsem,
    hsem,
    y_ss,
    ring_ss,
    rsem,
    ry_ss,
    ry_rs,
    rz_ss,
    rz_rs,
):
    sections, ny, nz, width = sizes
    tok = own_h.shape[2]
    tiles = ev_h.shape[1]
    rows = tok // tiles
    feats = w_h.shape[1]
    hd = ga_h.shape[3]
    s = lax.axis_index("section")
    t = lax.axis_index("tp")
    y, z = t // nz, t % nz
    before = (s + sections - 1) % sections
    after = (s + 1) % sections
    across = (s + sections // 2) % sections
    right = y * nz + (z + 1) % nz
    left = y * nz + (z + nz - 1) % nz

    def dev(section, tp):
        return {"section": section, "tp": tp}

    barrier = pltpu.get_barrier_semaphore()
    sources = [dev(across, t), dev(s, right), dev(s, left)]
    sources += [dev(s, ((y + i) % ny) * nz + z) for i in range(1, ny)]
    sources += [dev(after, y * nz + (z + i) % nz) for i in range(nz)]
    for d in sources:
        pl.semaphore_signal(barrier, inc=1, device_id=d, device_id_type=MESH)

    local = [
        pltpu.make_async_copy(own_h.at[0, 0], own_v, lsem.at[0]),
        pltpu.make_async_copy(ga_h.at[0, 0], ga_v, lsem.at[1]),
        pltpu.make_async_copy(ev_h, ev_s, lsem.at[2]),
        pltpu.make_async_copy(x_h.at[0], x_v, lsem.at[3]),
        pltpu.make_async_copy(gain_h, gain_v, lsem.at[4]),
        pltpu.make_async_copy(w_h.at[0], w_v, lsem.at[5]),
    ]
    for c in local:
        c.start()
    pl.semaphore_wait(barrier, len(sources))

    def remote(src, dst, send, recv, d):
        return pltpu.make_async_remote_copy(
            src_ref=src, dst_ref=dst, send_sem=send, recv_sem=recv, device_id=d, device_id_type=MESH
        )

    spare_c = remote(spare_h.at[0, 0], spare_v, hsem.at[0], hsem.at[1], dev(across, t))
    spare_c.start()
    x_c = remote(x_h.at[0], xr_v, hsem.at[2], hsem.at[3], dev(before, t))
    x_c.start()

    for c in local[:5]:
        c.wait()

    def token_row(v):
        half = v[:, :128]
        for i in range(128, feats, 128):
            half = half + v[:, i : i + 128]
        return jnp.sum(half.T, axis=0, keepdims=True)

    xf = x_v[...].astype(jnp.float32)
    red_loc[...] = jnp.zeros(red_loc.shape, jnp.float32)
    red_loc[0:1, :] = token_row(xf * xf)

    spare_c.wait_recv()
    parts = []
    for i in range(tiles):
        flag = jnp.full((rows, tok), ev_s[0, i], jnp.int32)
        parts.append(
            jnp.where(
                flag == 1,
                spare_v[i * rows : (i + 1) * rows, :].astype(jnp.float32),
                own_v[i * rows : (i + 1) * rows, :].astype(jnp.float32),
            )
        )
    mixed = jnp.concatenate(parts, axis=0)
    turned = mixed.T.astype(jnp.bfloat16)
    gath[t] = jnp.dot(turned, ga_v[...], preferred_element_type=jnp.float32).astype(jnp.bfloat16)

    def along(j, way):
        return remote(gath.at[j], gath.at[j], ring_ss.at[way, j], rsem.at[j], dev(s, (right, left)[way]))

    def arrived(j):
        along(j, 0).wait_recv()

    def peer(i):
        return ((y + i) % ny) * nz + z

    def share(i):
        return remote(gath.at[t], gath.at[t], y_ss.at[i], rsem.at[t], dev(s, peer(i)))

    along(t, 0).start()
    along(t, 1).start()
    for i in range(1, ny):
        share(i).start()
    local[5].wait()
    for i in range(1, ny):
        arrived(peer(i))
        along(peer(i), 0).start()
        along(peer(i), 1).start()

    def product(heads):
        lhs = jnp.concatenate([gath[j] for j in heads], axis=1)
        rhs = jnp.concatenate([w_v[:, pl.ds(pl.multiple_of(j * hd, hd), hd)] for j in heads], axis=1)
        return lax.dot_general(lhs, rhs, (((1,), (1,)), ((), ())), preferred_element_type=jnp.float32)

    acc[...] = product([peer(i) for i in range(ny)])

    half = nz // 2

    def step(k, last):
        from_left = (z + nz - k) % nz
        from_right = (z + k) % nz
        heads = []
        for i in range(ny):
            base = ((y + i) % ny) * nz
            arrived(base + from_left)
            if not last or i % 2 == 0:
                along(base + from_left, 0).start()
            arrived(base + from_right)
            if not last or i % 2 == 1:
                along(base + from_right, 1).start()
            heads += [base + from_left, base + from_right]
        acc[...] += product(heads)

    def middle(k, carry):
        step(k, False)
        return carry

    lax.fori_loop(1, half - 1, middle, 0)
    step(half - 1, True)
    far = [((y + i) % ny) * nz + (z + half) % nz for i in range(ny)]
    for j in far:
        arrived(j)

    scaled = (acc[...] + product(far)) * gain_v[...]
    a_send[...] = scaled.astype(jnp.bfloat16)
    red_loc[1:2, :] = token_row(scaled * xf)
    red_y[y] = red_loc[...]

    def over_y(i):
        return remote(red_loc, red_y.at[y], ry_ss.at[i], ry_rs.at[y], dev(s, peer(i)))

    def over_y_from(i):
        src = (y + i) % ny
        return remote(red_loc, red_y.at[src], ry_ss.at[i], ry_rs.at[src], dev(s, peer(i)))

    for i in range(1, ny):
        over_y(i).start()
    a_c = remote(a_send, a_recv, hsem.at[4], hsem.at[5], dev(before, t))
    a_c.start()
    for i in range(1, ny):
        over_y_from(i).wait_recv()
    total = red_y[0]
    for i in range(1, ny):
        total = total + red_y[i]
    red_col[...] = total

    def over_z(i):
        return remote(red_col, red_z.at[z], rz_ss.at[i], rz_rs.at[z], dev(before, y * nz + (z + i) % nz))

    def over_z_from(i):
        return remote(red_col, red_z.at[i], rz_ss.at[i], rz_rs.at[i], dev(before, t))

    for i in range(nz):
        over_z(i).start()
    x_c.wait_recv()
    a_c.wait_recv()
    for i in range(nz):
        over_z_from(i).wait_recv()
    total = red_z[0]
    for i in range(1, nz):
        total = total + red_z[i]
    inv = 1.0 / jnp.sqrt(total[0:1, :] / width + 1e-05)
    pull = total[1:2, :] * inv * inv * inv / width
    inv_c = jnp.broadcast_to(inv, (tok, tok)).T
    pull_c = jnp.broadcast_to(pull, (tok, tok)).T
    for i in range(0, feats, 128):
        a = a_recv[:, i : i + 128].astype(jnp.float32)
        xi = xr_v[:, i : i + 128].astype(jnp.float32)
        out_ref[0, :, i : i + 128] = (a * inv_c - xi * pull_c).astype(jnp.bfloat16)

    spare_c.wait_send()
    x_c.wait_send()
    a_c.wait_send()
    for i in range(1, ny):
        share(i).wait_send()
        over_y(i).wait_send()
    for i in range(nz):
        over_z(i).wait_send()
    for i in range(ny):
        base = ((y + i) % ny) * nz
        for k in range(half):
            if k < half - 1 or i % 2 == 0:
                along(base + (z + nz - k) % nz, 0).wait_send()
            if k < half - 1 or i % 2 == 1:
                along(base + (z + k) % nz, 1).wait_send()


def per_device(grad_attn, w_value, probs_own, probs_spare, evicted, layer_input, gain):
    sections, tp = lax.axis_size("section"), lax.axis_size("tp")
    ny = RUN
    nz = tp // ny
    tok = probs_own.shape[2]
    hd = grad_attn.shape[3]
    feats = w_value.shape[1]
    bf16, f32 = jnp.bfloat16, jnp.float32
    dma = pltpu.SemaphoreType.DMA
    return pl.pallas_call(
        functools.partial(kernel, (sections, ny, nz, feats * tp)),
        out_shape=jax.ShapeDtypeStruct(layer_input.shape, bf16),
        in_specs=[pl.BlockSpec(memory_space=pl.ANY)] * 7,
        out_specs=pl.BlockSpec(memory_space=pltpu.VMEM),
        scratch_shapes=[
            pltpu.VMEM((tok, hd), bf16),
            pltpu.VMEM(w_value.shape[1:], bf16),
            pltpu.VMEM((tok, tok), bf16),
            pltpu.VMEM((tok, tok), bf16),
            pltpu.SMEM(evicted.shape, jnp.int32),
            pltpu.VMEM((tok, feats), bf16),
            pltpu.VMEM((1, feats), f32),
            pltpu.VMEM((tok, feats), bf16),
            pltpu.VMEM((tp, tok, hd), bf16),
            pltpu.VMEM((tok, feats), f32),
            pltpu.VMEM((tok, feats), bf16),
            pltpu.VMEM((tok, feats), bf16),
            pltpu.VMEM((8, tok), f32),
            pltpu.VMEM((ny, 8, tok), f32),
            pltpu.VMEM((8, tok), f32),
            pltpu.VMEM((nz, 8, tok), f32),
            dma((6,)),
            dma((6,)),
            dma((ny,)),
            dma((2, tp)),
            dma((tp,)),
            dma((ny,)),
            dma((ny,)),
            dma((nz,)),
            dma((nz,)),
        ],
        compiler_params=pltpu.CompilerParams(collective_id=0, has_side_effects=True),
    )(grad_attn, w_value, probs_own, probs_spare, evicted, layer_input, gain)


def solution(mesh):
    in_specs = (
        P("section", "tp", None, None),
        P("section", "tp", None),
        P("section", "tp", None, None),
        P("section", "tp", None, None),
        P("section", None),
        P("section", None, "tp"),
        P("section", "tp"),
    )
    return jax.shard_map(
        per_device, mesh=mesh, in_specs=in_specs, out_specs=P("section", None, "tp"), check_vma=False
    )
```

time: 600 us -> 67.4 us (0.11)
  waiting for transfers between devices: 421 us -> 0 us
  blocking collectives: 94.7 us -> 0 us
  Pallas kernels: 0 us -> 65.8 us
  starting transfers between devices: 60.7 us -> 0 us
  between operations: 13.5 us -> 0.01 us
    all_gather x2 -> x0, waiting for transfers between devices: 416 us -> none  [the longest x1 222 us: per_device(): lax.all_gather(mixed, 'tp', axis=0, tiled=True)]
    psum x1 -> x0, blocking collectives: 94.7 us -> none  [per_device(): inner = lax.psum(local_inner, 'tp')]
    pallas_call x0 -> x1, Pallas kernels: none -> 65.8 us  [per_device(): pl.pallas_call(functools.partial(kernel, (sections, ny, nz, feats * tp)),...]
    ppermute x2 -> x0, starting transfers between devices: 60.6 us -> none  [passed_along(): return lax.ppermute(block, axis, route)]
  transfers between devices with their start and end apart: 4 -> 0, of which waited for: 4 -> 0; matrix products, arithmetic and copies ran while one was open for 1% -> 0% of each run, Pallas kernels for 0% -> 0%
where the time goes in v1:
time: 67.4 us; the launch traced here: 67.3 us
  Pallas kernels  65.8 us (98%)
  local copies, waits for them, and re-layouts  1.47 us (2%)
    pallas_call x1, Pallas kernels, per_device(): pl.pallas_call(functools.partial(kernel, (sections, ny, nz, feats * tp)),...  65.8 us
    unnamed x1, local copies, waits for them, and re-layouts  1.47 us

profile of v1, /device:TPU:1, one launch (start us, length us, event | category | flops | bytes accessed | tf_op | source)
XLA Modules:
  0.0 67.3 jit_solution(15914553506210330553)
XLA Ops:
  0.0 65.8 %shard_map.73 = bf16[1,128,256]{2,1,0:T(8,128)(2,1)} custom-call(bf16[1,1,128,128]{3,2,1,0:T(8,128)(2,1)} %ga_h.1, bf16[1,256,6144]{2,1,0:T(8,128)(2,1)} %w_h.1, bf16[1,1,128,128]{3,2,1,0:T(8,128)(2,1)} %own_h.1, bf16[1,1,128,128]{3,2,1,0:T(8,128)(2,1)} %spare_h.1, s32[1,4]{1,0:T(1,128)} %ev_h.1, bf16[1,128,256]{2,1,0:T(8,128)(2,1)} %x_h.1, f32[1,256]{1,0:T(1,128)} %gain_h.1), custom_call_target="tpu_custom_call" | custom-call | tf_op jit(solution)/shard_map/pallas_call | solution.py:254
  65.8 1.5 %copy.9 = bf16[1,128,256]{2,1,0:T(8,128)(2,1)} copy(bf16[1,128,256]{2,1,0:T(8,128)(2,1)} %shard_map.73) | data formatting | bytes 131072

commit v2 on v1

--- a/solution.py
+++ b/solution.py
@@ -1,4 +1,5 @@
 import functools
+import itertools
 
 import jax
 import jax.numpy as jnp
@@ -8,6 +9,7 @@
 from jax.sharding import PartitionSpec as P
 
 RUN = 4
+TREE = {0: (1,), 1: (2,), 2: (3,), 3: (4,), 4: (5, 6)}
 MESH = pl.DeviceIdType.MESH
 
 
@@ -34,9 +36,7 @@
     a_send,
     a_recv,
     red_loc,
-    red_y,
-    red_col,
-    red_z,
+    red_all,
     lsem,
     hsem,
     y_ss,
@@ -44,8 +44,6 @@
     rsem,
     ry_ss,
     ry_rs,
-    rz_ss,
-    rz_rs,
 ):
     sections, ny, nz, width = sizes
     tok = own_h.shape[2]
@@ -59,16 +57,15 @@
     before = (s + sections - 1) % sections
     after = (s + 1) % sections
     across = (s + sections // 2) % sections
-    right = y * nz + (z + 1) % nz
-    left = y * nz + (z + nz - 1) % nz
 
     def dev(section, tp):
         return {"section": section, "tp": tp}
 
     barrier = pltpu.get_barrier_semaphore()
-    sources = [dev(across, t), dev(s, right), dev(s, left)]
+    jumps = sorted({b - a for a, far in TREE.items() for b in far})
+    sources = [dev(across, t), dev(after, t)]
     sources += [dev(s, ((y + i) % ny) * nz + z) for i in range(1, ny)]
-    sources += [dev(after, y * nz + (z + i) % nz) for i in range(nz)]
+    sources += [dev(s, y * nz + (z + d) % nz) for j in jumps for d in (j, nz - j)]
     for d in sources:
         pl.semaphore_signal(barrier, inc=1, device_id=d, device_id_type=MESH)
 
@@ -92,7 +89,6 @@
     spare_c = remote(spare_h.at[0, 0], spare_v, hsem.at[0], hsem.at[1], dev(across, t))
     spare_c.start()
     x_c = remote(x_h.at[0], xr_v, hsem.at[2], hsem.at[3], dev(before, t))
-    x_c.start()
 
     for c in local[:5]:
         c.wait()
@@ -122,11 +118,7 @@
     turned = mixed.T.astype(jnp.bfloat16)
     gath[t] = jnp.dot(turned, ga_v[...], preferred_element_type=jnp.float32).astype(jnp.bfloat16)
 
-    def along(j, way):
-        return remote(gath.at[j], gath.at[j], ring_ss.at[way, j], rsem.at[j], dev(s, (right, left)[way]))
-
-    def arrived(j):
-        along(j, 0).wait_recv()
+    half = nz // 2
 
     def peer(i):
         return ((y + i) % ny) * nz + z
@@ -134,88 +126,82 @@
     def share(i):
         return remote(gath.at[t], gath.at[t], y_ss.at[i], rsem.at[t], dev(s, peer(i)))
 
-    along(t, 0).start()
-    along(t, 1).start()
-    for i in range(1, ny):
-        share(i).start()
-    local[5].wait()
-    for i in range(1, ny):
-        arrived(peer(i))
-        along(peer(i), 0).start()
-        along(peer(i), 1).start()
+    def block(i, k, way):
+        return ((y + i) % ny) * nz + ((z + nz - k) % nz if way == 0 else (z + k) % nz)
+
+    def comes(i, k, way):
+        return k < half or i % 2 == way
+
+    def onward(i, k, way):
+        j = block(i, k, way)
+        copies = []
+        for n, far in enumerate(TREE.get(k, ())):
+            if comes(i, far, way):
+                step = far - k
+                to = y * nz + ((z + step) % nz if way == 0 else (z + nz - step) % nz)
+                copies.append(remote(gath.at[j], gath.at[j], ring_ss.at[way, n, j], rsem.at[j], dev(s, to)))
+        return copies
+
+    def arrived(j):
+        remote(gath.at[j], gath.at[j], y_ss.at[0], rsem.at[j], dev(s, peer(1))).wait_recv()
 
     def product(heads):
         lhs = jnp.concatenate([gath[j] for j in heads], axis=1)
         rhs = jnp.concatenate([w_v[:, pl.ds(pl.multiple_of(j * hd, hd), hd)] for j in heads], axis=1)
         return lax.dot_general(lhs, rhs, (((1,), (1,)), ((), ())), preferred_element_type=jnp.float32)
 
+    def send_on(i, k):
+        for right_copy, left_copy in itertools.zip_longest(onward(i, k, 0), onward(i, k, 1)):
+            for c in (right_copy, left_copy):
+                if c is not None:
+                    c.start()
+
+    for i in range(1, ny):
+        share(i).start()
+    send_on(0, 0)
+    x_c.start()
+    local[5].wait()
+    for i in range(1, ny):
+        arrived(peer(i))
+        send_on(i, 0)
     acc[...] = product([peer(i) for i in range(ny)])
 
-    half = nz // 2
-
-    def step(k, last):
-        from_left = (z + nz - k) % nz
-        from_right = (z + k) % nz
+    depth = {0: 0}
+    for k in sorted(TREE):
+        for far in TREE[k]:
+            depth[far] = depth[k] + 1
+    for k in sorted(range(1, half + 1), key=lambda k: (depth[k], k not in TREE, k)):
         heads = []
         for i in range(ny):
-            base = ((y + i) % ny) * nz
-            arrived(base + from_left)
-            if not last or i % 2 == 0:
-                along(base + from_left, 0).start()
-            arrived(base + from_right)
-            if not last or i % 2 == 1:
-                along(base + from_right, 1).start()
-            heads += [base + from_left, base + from_right]
+            for way in range(2):
+                if comes(i, k, way):
+                    arrived(block(i, k, way))
+                    for c in onward(i, k, way):
+                        c.start()
+                    heads.append(block(i, k, way))
         acc[...] += product(heads)
 
-    def middle(k, carry):
-        step(k, False)
-        return carry
-
-    lax.fori_loop(1, half - 1, middle, 0)
-    step(half - 1, True)
-    far = [((y + i) % ny) * nz + (z + half) % nz for i in range(ny)]
-    for j in far:
-        arrived(j)
-
-    scaled = (acc[...] + product(far)) * gain_v[...]
+    scaled = acc[...] * gain_v[...]
     a_send[...] = scaled.astype(jnp.bfloat16)
     red_loc[1:2, :] = token_row(scaled * xf)
-    red_y[y] = red_loc[...]
-
-    def over_y(i):
-        return remote(red_loc, red_y.at[y], ry_ss.at[i], ry_rs.at[y], dev(s, peer(i)))
-
-    def over_y_from(i):
-        src = (y + i) % ny
-        return remote(red_loc, red_y.at[src], ry_ss.at[i], ry_rs.at[src], dev(s, peer(i)))
-
-    for i in range(1, ny):
-        over_y(i).start()
+
+    def share_sum(i, k):
+        to = ((y + i) % ny) * nz + (z + k) % nz
+        return remote(red_loc, red_all.at[t], ry_ss.at[i, k], ry_rs.at[t], dev(before, to))
+
+    def share_sum_from(j):
+        return remote(red_loc, red_all.at[j], ry_ss.at[0, 0], ry_rs.at[j], dev(before, t))
+
+    for k in sorted(range(nz), key=lambda k: -min(k, nz - k)):
+        for i in range(ny):
+            share_sum(i, k).start()
     a_c = remote(a_send, a_recv, hsem.at[4], hsem.at[5], dev(before, t))
     a_c.start()
-    for i in range(1, ny):
-        over_y_from(i).wait_recv()
-    total = red_y[0]
-    for i in range(1, ny):
-        total = total + red_y[i]
-    red_col[...] = total
-
-    def over_z(i):
-        return remote(red_col, red_z.at[z], rz_ss.at[i], rz_rs.at[z], dev(before, y * nz + (z + i) % nz))
-
-    def over_z_from(i):
-        return remote(red_col, red_z.at[i], rz_ss.at[i], rz_rs.at[i], dev(before, t))
-
-    for i in range(nz):
-        over_z(i).start()
     x_c.wait_recv()
     a_c.wait_recv()
-    for i in range(nz):
-        over_z_from(i).wait_recv()
-    total = red_z[0]
-    for i in range(1, nz):
-        total = total + red_z[i]
+    for j in range(ny * nz):
+        share_sum_from(j).wait_recv()
+    total = jnp.sum(red_all[...], axis=0)
     inv = 1.0 / jnp.sqrt(total[0:1, :] / width + 1e-05)
     pull = total[1:2, :] * inv * inv * inv / width
     inv_c = jnp.broadcast_to(inv, (tok, tok)).T
@@ -230,16 +216,14 @@
     a_c.wait_send()
     for i in range(1, ny):
         share(i).wait_send()
-        over_y(i).wait_send()
-    for i in range(nz):
-        over_z(i).wait_send()
     for i in range(ny):
-        base = ((y + i) % ny) * nz
-        for k in range(half):
-            if k < half - 1 or i % 2 == 0:
-                along(base + (z + nz - k) % nz, 0).wait_send()
-            if k < half - 1 or i % 2 == 1:
-                along(base + (z + k) % nz, 1).wait_send()
+        for k in range(nz):
+            share_sum(i, k).wait_send()
+    for i in range(ny):
+        for k in TREE:
+            for way in range(2):
+                for c in onward(i, k, way):
+                    c.wait_send()
 
 
 def per_device(grad_attn, w_value, probs_own, probs_spare, evicted, layer_input, gain):
@@ -269,19 +253,15 @@
             pltpu.VMEM((tok, feats), f32),
             pltpu.VMEM((tok, feats), bf16),
             pltpu.VMEM((tok, feats), bf16),
-            pltpu.VMEM((8, tok), f32),
-            pltpu.VMEM((ny, 8, tok), f32),
-            pltpu.VMEM((8, tok), f32),
-            pltpu.VMEM((nz, 8, tok), f32),
+            pltpu.VMEM((2, tok), f32),
+            pltpu.VMEM((tp, 2, tok), f32),
             dma((6,)),
             dma((6,)),
             dma((ny,)),
-            dma((2, tp)),
+            dma((2, max(len(far) for far in TREE.values()), tp)),
             dma((tp,)),
-            dma((ny,)),
-            dma((ny,)),
-            dma((nz,)),
-            dma((nz,)),
+            dma((ny, nz)),
+            dma((tp,)),
         ],
         compiler_params=pltpu.CompilerParams(collective_id=0, has_side_effects=True),
     )(grad_attn, w_value, probs_own, probs_spare, evicted, layer_input, gain)

time: 67.4 us -> 60.5 us (0.90)
  Pallas kernels: 65.8 us -> 58.8 us
    pallas_call x1, Pallas kernels: 65.8 us -> 58.8 us  [per_device(): pl.pallas_call(functools.partial(kernel, (sections, ny, nz, feats * tp)),...]
where the time goes in v2:
time: 60.5 us; the launch traced here: 60.3 us
  Pallas kernels  58.8 us (97%)
  local copies, waits for them, and re-layouts  1.47 us (2%)
    pallas_call x1, Pallas kernels, per_device(): pl.pallas_call(functools.partial(kernel, (sections, ny, nz, feats * tp)),...  58.8 us
    unnamed x1, local copies, waits for them, and re-layouts  1.47 us

profile of v2, /device:TPU:1, one launch (start us, length us, event | category | flops | bytes accessed | tf_op | source)
XLA Modules:
  0.0 60.3 jit_solution(7570754488630327925)
XLA Ops:
  0.0 58.8 %shard_map.73 = bf16[1,128,256]{2,1,0:T(8,128)(2,1)} custom-call(bf16[1,1,128,128]{3,2,1,0:T(8,128)(2,1)} %ga_h.1, bf16[1,256,6144]{2,1,0:T(8,128)(2,1)} %w_h.1, bf16[1,1,128,128]{3,2,1,0:T(8,128)(2,1)} %own_h.1, bf16[1,1,128,128]{3,2,1,0:T(8,128)(2,1)} %spare_h.1, s32[1,4]{1,0:T(1,128)} %ev_h.1, bf16[1,128,256]{2,1,0:T(8,128)(2,1)} %x_h.1, f32[1,256]{1,0:T(1,128)} %gain_h.1), custom_call_target="tpu_custom_call" | custom-call | tf_op jit(solution)/shard_map/pallas_call | solution.py:238
  58.8 1.5 %copy.9 = bf16[1,128,256]{2,1,0:T(8,128)(2,1)} copy(bf16[1,128,256]{2,1,0:T(8,128)(2,1)} %shard_map.73) | data formatting | bytes 131072

commit v3 on v2

--- a/solution.py
+++ b/solution.py
@@ -9,7 +9,9 @@
 from jax.sharding import PartitionSpec as P
 
 RUN = 4
-TREE = {0: (1,), 1: (2,), 2: (3,), 3: (4,), 4: (5, 6)}
+TREE = {0: (2, 1), 2: (4, 3), 4: (5, 6)}
+BOTH = (1,)
+WIDEST = max(len(far) for far in TREE.values())
 MESH = pl.DeviceIdType.MESH
 
 
@@ -64,7 +66,9 @@
     barrier = pltpu.get_barrier_semaphore()
     jumps = sorted({b - a for a, far in TREE.items() for b in far})
     sources = [dev(across, t), dev(after, t)]
-    sources += [dev(s, ((y + i) % ny) * nz + z) for i in range(1, ny)]
+    beside = y + 1 - 2 * (y % 2)
+    rows_of = [y, beside, (y + 2) % ny, (beside + 2) % ny]
+    sources += [dev(s, rows_of[i] * nz + z) for i in range(1, ny)]
     sources += [dev(s, y * nz + (z + d) % nz) for j in jumps for d in (j, nz - j)]
     for d in sources:
         pl.semaphore_signal(barrier, inc=1, device_id=d, device_id_type=MESH)
@@ -89,6 +93,8 @@
     spare_c = remote(spare_h.at[0, 0], spare_v, hsem.at[0], hsem.at[1], dev(across, t))
     spare_c.start()
     x_c = remote(x_h.at[0], xr_v, hsem.at[2], hsem.at[3], dev(before, t))
+
+    x_c.start()
 
     for c in local[:5]:
         c.wait()
@@ -121,25 +127,31 @@
     half = nz // 2
 
     def peer(i):
-        return ((y + i) % ny) * nz + z
+        return rows_of[i] * nz + z
 
     def share(i):
         return remote(gath.at[t], gath.at[t], y_ss.at[i], rsem.at[t], dev(s, peer(i)))
 
     def block(i, k, way):
-        return ((y + i) % ny) * nz + ((z + nz - k) % nz if way == 0 else (z + k) % nz)
+        return rows_of[i] * nz + ((z + nz - k) % nz if way == 0 else (z + k) % nz)
 
     def comes(i, k, way):
-        return k < half or i % 2 == way
+        return k < half or i // 2 == way
+
+    def travels(i, k):
+        return i % 2 == 0 or k in BOTH
 
     def onward(i, k, way):
         j = block(i, k, way)
         copies = []
         for n, far in enumerate(TREE.get(k, ())):
-            if comes(i, far, way):
+            if comes(i, far, way) and travels(i, far):
                 step = far - k
                 to = y * nz + ((z + step) % nz if way == 0 else (z + nz - step) % nz)
                 copies.append(remote(gath.at[j], gath.at[j], ring_ss.at[way, n, j], rsem.at[j], dev(s, to)))
+        if k and i % 2 == 0 and not travels(i + 1, k):
+            to = beside * nz + z
+            copies.append(remote(gath.at[j], gath.at[j], ring_ss.at[way, WIDEST, j], rsem.at[j], dev(s, to)))
         return copies
 
     def arrived(j):
@@ -156,12 +168,11 @@
                 if c is not None:
                     c.start()
 
-    for i in range(1, ny):
+    for i in (2, 1, 3):
         share(i).start()
     send_on(0, 0)
-    x_c.start()
     local[5].wait()
-    for i in range(1, ny):
+    for i in (2, 1, 3):
         arrived(peer(i))
         send_on(i, 0)
     acc[...] = product([peer(i) for i in range(ny)])
@@ -170,23 +181,31 @@
     for k in sorted(TREE):
         for far in TREE[k]:
             depth[far] = depth[k] + 1
-    for k in sorted(range(1, half + 1), key=lambda k: (depth[k], k not in TREE, k)):
+    order = sorted(range(1, half + 1), key=lambda k: (depth[k], k not in TREE, k))
+    handed = []
+    for k in order:
         heads = []
-        for i in range(ny):
+        for i in (0, 2, 1, 3):
             for way in range(2):
                 if comes(i, k, way):
-                    arrived(block(i, k, way))
-                    for c in onward(i, k, way):
-                        c.start()
-                    heads.append(block(i, k, way))
+                    if travels(i, k):
+                        arrived(block(i, k, way))
+                        for c in onward(i, k, way):
+                            c.start()
+                        heads.append(block(i, k, way))
+                    else:
+                        handed.append(block(i, k, way))
         acc[...] += product(heads)
+    for j in handed:
+        arrived(j)
+    acc[...] += product(handed)
 
     scaled = acc[...] * gain_v[...]
     a_send[...] = scaled.astype(jnp.bfloat16)
     red_loc[1:2, :] = token_row(scaled * xf)
 
     def share_sum(i, k):
-        to = ((y + i) % ny) * nz + (z + k) % nz
+        to = rows_of[i] * nz + (z + k) % nz
         return remote(red_loc, red_all.at[t], ry_ss.at[i, k], ry_rs.at[t], dev(before, to))
 
     def share_sum_from(j):
@@ -220,10 +239,11 @@
         for k in range(nz):
             share_sum(i, k).wait_send()
     for i in range(ny):
-        for k in TREE:
+        for k in range(half + 1):
             for way in range(2):
-                for c in onward(i, k, way):
-                    c.wait_send()
+                if comes(i, k, way) and (k == 0 or travels(i, k)):
+                    for c in onward(i, k, way):
+                        c.wait_send()
 
 
 def per_device(grad_attn, w_value, probs_own, probs_spare, evicted, layer_input, gain):
@@ -258,7 +278,7 @@
             dma((6,)),
             dma((6,)),
             dma((ny,)),
-            dma((2, max(len(far) for far in TREE.values()), tp)),
+            dma((2, WIDEST + 1, tp)),
             dma((tp,)),
             dma((ny, nz)),
             dma((tp,)),

time: 60.5 us -> 58.3 us (0.964)
  Pallas kernels: 58.8 us -> 56.6 us
    pallas_call x1, Pallas kernels: 58.8 us -> 56.6 us  [per_device(): pl.pallas_call(functools.partial(kernel, (sections, ny, nz, feats * tp)),...]
where the time goes in v3:
time: 58.3 us; the launch traced here: 58.1 us
  Pallas kernels  56.6 us (97%)
  local copies, waits for them, and re-layouts  1.47 us (3%)
    pallas_call x1, Pallas kernels, per_device(): pl.pallas_call(functools.partial(kernel, (sections, ny, nz, feats * tp)),...  56.6 us
    unnamed x1, local copies, waits for them, and re-layouts  1.47 us

profile of v3, /device:TPU:1, one launch (start us, length us, event | category | flops | bytes accessed | tf_op | source)
XLA Modules:
  0.0 58.1 jit_solution(2229566952794102339)
XLA Ops:
  0.0 56.6 %shard_map.73 = bf16[1,128,256]{2,1,0:T(8,128)(2,1)} custom-call(bf16[1,1,128,128]{3,2,1,0:T(8,128)(2,1)} %ga_h.1, bf16[1,256,6144]{2,1,0:T(8,128)(2,1)} %w_h.1, bf16[1,1,128,128]{3,2,1,0:T(8,128)(2,1)} %own_h.1, bf16[1,1,128,128]{3,2,1,0:T(8,128)(2,1)} %spare_h.1, s32[1,4]{1,0:T(1,128)} %ev_h.1, bf16[1,128,256]{2,1,0:T(8,128)(2,1)} %x_h.1, f32[1,256]{1,0:T(1,128)} %gain_h.1), custom_call_target="tpu_custom_call" | custom-call | tf_op jit(solution)/shard_map/pallas_call | solution.py:258
  56.6 1.5 %copy.9 = bf16[1,128,256]{2,1,0:T(8,128)(2,1)} copy(bf16[1,128,256]{2,1,0:T(8,128)(2,1)} %shard_map.73) | data formatting | bytes 131072

commit v4 on v3

--- a/solution.py
+++ b/solution.py
@@ -11,6 +11,7 @@
 RUN = 4
 TREE = {0: (2, 1), 2: (4, 3), 4: (5, 6)}
 BOTH = (1,)
+BEHIND = 2
 WIDEST = max(len(far) for far in TREE.values())
 MESH = pl.DeviceIdType.MESH
 
@@ -182,9 +183,9 @@
         for far in TREE[k]:
             depth[far] = depth[k] + 1
     order = sorted(range(1, half + 1), key=lambda k: (depth[k], k not in TREE, k))
-    handed = []
+    waiting = []
     for k in order:
-        heads = []
+        heads, handed = [], []
         for i in (0, 2, 1, 3):
             for way in range(2):
                 if comes(i, k, way):
@@ -195,10 +196,17 @@
                         heads.append(block(i, k, way))
                     else:
                         handed.append(block(i, k, way))
+        waiting.append(handed)
+        if len(waiting) > BEHIND:
+            for j in waiting[0]:
+                arrived(j)
+            heads += waiting.pop(0)
         acc[...] += product(heads)
-    for j in handed:
-        arrived(j)
-    acc[...] += product(handed)
+    for handed in waiting:
+        for j in handed:
+            arrived(j)
+        if handed:
+            acc[...] += product(handed)
 
     scaled = acc[...] * gain_v[...]
     a_send[...] = scaled.astype(jnp.bfloat16)

time: 58.3 us -> 57.7 us (0.990)
  Pallas kernels: 56.6 us -> 56 us
    pallas_call x1, Pallas kernels: 56.6 us -> 56 us  [per_device(): pl.pallas_call(functools.partial(kernel, (sections, ny, nz, feats * tp)),...]
where the time goes in v4:
time: 57.7 us; the launch traced here: 57.5 us
  Pallas kernels  56 us (97%)
  local copies, waits for them, and re-layouts  1.47 us (3%)
    pallas_call x1, Pallas kernels, per_device(): pl.pallas_call(functools.partial(kernel, (sections, ny, nz, feats * tp)),...  56 us
    unnamed x1, local copies, waits for them, and re-layouts  1.47 us

profile of v4, /device:TPU:1, one launch (start us, length us, event | category | flops | bytes accessed | tf_op | source)
XLA Modules:
  0.0 57.5 jit_solution(9693683773018708591)
XLA Ops:
  0.0 56.0 %shard_map.73 = bf16[1,128,256]{2,1,0:T(8,128)(2,1)} custom-call(bf16[1,1,128,128]{3,2,1,0:T(8,128)(2,1)} %ga_h.1, bf16[1,256,6144]{2,1,0:T(8,128)(2,1)} %w_h.1, bf16[1,1,128,128]{3,2,1,0:T(8,128)(2,1)} %own_h.1, bf16[1,1,128,128]{3,2,1,0:T(8,128)(2,1)} %spare_h.1, s32[1,4]{1,0:T(1,128)} %ev_h.1, bf16[1,128,256]{2,1,0:T(8,128)(2,1)} %x_h.1, f32[1,256]{1,0:T(1,128)} %gain_h.1), custom_call_target="tpu_custom_call" | custom-call | tf_op jit(solution)/shard_map/pallas_call | solution.py:266
  56.0 1.5 %copy.9 = bf16[1,128,256]{2,1,0:T(8,128)(2,1)} copy(bf16[1,128,256]{2,1,0:T(8,128)(2,1)} %shard_map.73) | data formatting | bytes 131072

commit v5 on v4

--- a/solution.py
+++ b/solution.py
@@ -210,6 +210,8 @@
 
     scaled = acc[...] * gain_v[...]
     a_send[...] = scaled.astype(jnp.bfloat16)
+    a_c = remote(a_send, a_recv, hsem.at[4], hsem.at[5], dev(before, t))
+    a_c.start()
     red_loc[1:2, :] = token_row(scaled * xf)
 
     def share_sum(i, k):
@@ -222,8 +224,6 @@
     for k in sorted(range(nz), key=lambda k: -min(k, nz - k)):
         for i in range(ny):
             share_sum(i, k).start()
-    a_c = remote(a_send, a_recv, hsem.at[4], hsem.at[5], dev(before, t))
-    a_c.start()
     x_c.wait_recv()
     a_c.wait_recv()
     for j in range(ny * nz):

time: 57.7 us -> 57.7 us (level)
  no operation moved by 1% of the time
where the time goes in v5:
time: 57.7 us; the launch traced here: 57.5 us
  Pallas kernels  56 us (97%)
  local copies, waits for them, and re-layouts  1.47 us (3%)
    pallas_call x1, Pallas kernels, per_device(): pl.pallas_call(functools.partial(kernel, (sections, ny, nz, feats * tp)),...  56 us
    unnamed x1, local copies, waits for them, and re-layouts  1.47 us

profile of v5, /device:TPU:1, one launch (start us, length us, event | category | flops | bytes accessed | tf_op | source)
XLA Modules:
  0.0 57.5 jit_solution(13085212065338067784)
XLA Ops:
  0.0 56.0 %shard_map.73 = bf16[1,128,256]{2,1,0:T(8,128)(2,1)} custom-call(bf16[1,1,128,128]{3,2,1,0:T(8,128)(2,1)} %ga_h.1, bf16[1,256,6144]{2,1,0:T(8,128)(2,1)} %w_h.1, bf16[1,1,128,128]{3,2,1,0:T(8,128)(2,1)} %own_h.1, bf16[1,1,128,128]{3,2,1,0:T(8,128)(2,1)} %spare_h.1, s32[1,4]{1,0:T(1,128)} %ev_h.1, bf16[1,128,256]{2,1,0:T(8,128)(2,1)} %x_h.1, f32[1,256]{1,0:T(1,128)} %gain_h.1), custom_call_target="tpu_custom_call" | custom-call | tf_op jit(solution)/shard_map/pallas_call | solution.py:266
  56.0 1.5 %copy.9 = bf16[1,128,256]{2,1,0:T(8,128)(2,1)} copy(bf16[1,128,256]{2,1,0:T(8,128)(2,1)} %shard_map.73) | data formatting | bytes 131072
